TPU v7x, 32 devices: a whole 2x2x4 slice. The times are simulated.
32 devices in a mesh: blk: 8 (over y, x, core), req: 4 (over z).
Axes of the slice: x: 2, y: 2, z: 4, core: 2. Of those that a mesh axis runs over, the one named last changes fastest.
Arguments:
- verified_queries: bfloat16 [4, 16, 5, 1024], P('req', 'blk'), may hold values from -96 to 96
- new_keys: bfloat16 [4, 16, 5, 256], P('req', 'blk'), may hold values from -6 to 6
- verified_value_rows: bfloat16 [4, 16, 5, 256], P('req', 'blk'), may hold values from -6 to 6
- prior_round_keys: bfloat16 [4, 16, 5, 256], P('req', 'blk'), may hold values from -6 to 6
- prior_round_values: bfloat16 [4, 16, 5, 256], P('req', 'blk'), may hold values from -6 to 6
- accepted: int32 [4, 16], P('req', 'blk'), may hold values from 0 to 5
- group_id: int32 [4, 16], P('req'), may hold values from 0 to 15
- cache_len: int32 [4, 16], P('req'), may hold values from 0 to 8192, as said below
- slot_owner: int32 [4, 64], P('req'), may hold values from 0 to 15, as said below
- piece_cache_keys: bfloat16 [4, 64, 256, 256], P('req', 'blk'), may hold values from -6 to 6
- piece_cache_values: bfloat16 [4, 64, 256, 256], P('req', 'blk'), may hold values from -6 to 6
- shared_prompt_keys: bfloat16 [16, 256, 256], P('req', 'blk'), may hold values from -6 to 6
- shared_prompt_values: bfloat16 [16, 256, 256], P('req', 'blk'), may hold values from -6 to 6
- prompt_mask: int32 [16, 8], P('req', 'blk'), may hold values 0 or 1
Outputs:
- attended: bfloat16 [4, 16, 5, 1024], P('req', 'blk')
Inputs may be any that keep to these rules, and one draw needn't show every extreme that they name: `slot_owner`: A request's cache is the concatenation, in piece order, of the pieces that name it. In every batch one request owns exactly 32 pieces and no request owns more. `cache_len`: A request's length is at most 256 times the number of pieces it owns and more than 256 times one fewer; in every batch one request holds exactly 8192 rows.
All inputs are finite; a program needn't handle non-finite values. No bound on the sum of `prompt_mask` on one device may be relied on, other than what follows from the above.
Results may differ from a plain program's by a relative error of at most 0.003.
Values may be sent and summed in bfloat16 or wider, within the bound.
No kernel may reach another device: no remote copies, remote signals or barrier semaphores. Data moves between devices by JAX's collectives and lax.ppermute only.
A program may use at most 64 MiB of HBM per device.

v0:
```python
import jax
import jax.numpy as jnp
from jax import lax
from jax.sharding import PartitionSpec as P

QUERY_HEADS = 16
KEY_HEADS = 4
HEAD_SIZE = 64
VERIFIED_COUNT = 5
LOWEST = -1e30


def block_weights(scores, live_rows):
    masked = jnp.where(live_rows, scores, LOWEST)
    ceiling = jnp.max(masked, axis=-1)
    weights = jnp.where(live_rows, jnp.exp(masked - ceiling[..., None]), 0.0).astype(jnp.bfloat16)
    return (ceiling, weights, jnp.sum(weights.astype(jnp.float32), axis=-1))


def per_device(
    verified_queries,
    new_keys,
    verified_value_rows,
    prior_round_keys,
    prior_round_values,
    accepted,
    group_id,
    cache_len,
    slot_owner,
    piece_cache_keys,
    piece_cache_values,
    shared_prompt_keys,
    shared_prompt_values,
    prompt_mask,
):
    position_here = lax.axis_index("blk")
    request_rows = verified_queries.shape[1]
    rows_of_batch = group_id.shape[1]
    local_pieces = piece_cache_keys.shape[1]
    rows_of_piece = piece_cache_keys.shape[2]
    heads_per_key = QUERY_HEADS // KEY_HEADS
    score_scale = HEAD_SIZE ** (-0.5)
    row_lanes = QUERY_HEADS * VERIFIED_COUNT
    highest = lax.Precision.HIGHEST
    every_query = lax.all_gather(verified_queries, "blk", axis=1, tiled=True)[0].reshape(
        rows_of_batch, VERIFIED_COUNT, KEY_HEADS, heads_per_key, HEAD_SIZE
    )
    owners = slot_owner[0]
    requests_all = jnp.arange(rows_of_batch, dtype=jnp.int32)
    owner_table = (owners[:, None] == requests_all[None, :]).astype(jnp.int32)
    before = jnp.cumsum(owner_table, axis=0) - owner_table
    ranking = jnp.sum(before * owner_table, axis=1)
    filling = jnp.clip(cache_len[0][owners] - ranking * rows_of_piece, 0, rows_of_piece)
    my_owner = lax.dynamic_slice_in_dim(owners, position_here * local_pieces, local_pieces)
    my_fill = lax.dynamic_slice_in_dim(filling, position_here * local_pieces, local_pieces)
    slot_query = every_query[my_owner]
    keys_of_slot = piece_cache_keys[0].reshape(local_pieces, rows_of_piece, KEY_HEADS, HEAD_SIZE)
    values_of_slot = piece_cache_values[0].reshape(
        local_pieces, rows_of_piece, KEY_HEADS, HEAD_SIZE
    )
    scores = (
        jnp.einsum(
            "snkgd,sjkd->skgnj", slot_query, keys_of_slot, preferred_element_type=jnp.float32
        )
        * score_scale
    )
    live_piece = jnp.arange(rows_of_piece, dtype=jnp.int32)[None, :] < my_fill[:, None]
    live_rows = jnp.broadcast_to(live_piece[:, None, None, None, :], scores.shape)
    slot_top, slot_weights, slot_mass = block_weights(scores, live_rows)
    slot_part = jnp.einsum(
        "skgnj,sjkd->skgnd", slot_weights, values_of_slot, preferred_element_type=jnp.float32
    )
    collected_keys, collected_values, gathered_live = (
        lax.all_gather(shared_prompt_keys, "req", axis=0, tiled=True),
        lax.all_gather(shared_prompt_values, "req", axis=0, tiled=True),
        lax.all_gather(prompt_mask[:, 0].astype(jnp.bfloat16), "req", axis=0, tiled=True),
    )
    prompt_groups = group_id[0]
    keys_of_block = collected_keys[prompt_groups].reshape(rows_of_batch, -1, KEY_HEADS, HEAD_SIZE)
    values_of_block = collected_values[prompt_groups].reshape(
        rows_of_batch, -1, KEY_HEADS, HEAD_SIZE
    )
    block_live = gathered_live[prompt_groups] > 0.5
    scores = (
        jnp.einsum(
            "rnkgd,rjkd->rkgnj", every_query, keys_of_block, preferred_element_type=jnp.float32
        )
        * score_scale
    )
    live_rows = jnp.broadcast_to(block_live[:, None, None, None, None], scores.shape)
    prompt_top, prompt_weights, prompt_mass = block_weights(scores, live_rows)
    prompt_part = jnp.einsum(
        "rkgnj,rjkd->rkgnd", prompt_weights, values_of_block, preferred_element_type=jnp.float32
    )
    choose = my_owner[:, None] == requests_all[None, :]
    picked = choose.astype(jnp.float32)
    slot_flat = slot_top.reshape(local_pieces, row_lanes)
    prompt_flat = prompt_top.reshape(rows_of_batch, row_lanes)
    slot_best = jnp.max(jnp.where(choose[:, :, None], slot_flat[:, None, :], LOWEST), axis=0)
    device_top = jnp.maximum(slot_best, prompt_flat)
    overall_top = lax.pmax(device_top, "blk")
    slot_lift = jnp.exp(slot_flat - overall_top[my_owner])
    slot_terms = (
        slot_lift[..., None] * slot_part.reshape(local_pieces, row_lanes, HEAD_SIZE)
    ).reshape(local_pieces, row_lanes * HEAD_SIZE)
    prompt_lift = jnp.exp(prompt_flat - overall_top)
    numerator = jnp.dot(picked.T, slot_terms, precision=highest) + (
        prompt_lift[..., None] * prompt_part.reshape(rows_of_batch, row_lanes, HEAD_SIZE)
    ).reshape(rows_of_batch, row_lanes * HEAD_SIZE)
    denominator = jnp.dot(
        picked.T, slot_lift * slot_mass.reshape(local_pieces, row_lanes), precision=highest
    ) + prompt_lift * prompt_mass.reshape(rows_of_batch, row_lanes)
    numerator, denominator = (numerator, denominator)
    got_numerator, got_denominator = (
        lax.psum_scatter(numerator, "blk", scatter_dimension=0, tiled=True),
        lax.psum_scatter(denominator, "blk", scatter_dimension=0, tiled=True),
    )
    got_top = lax.dynamic_slice_in_dim(overall_top, position_here * request_rows, request_rows)
    request_query = verified_queries[0].reshape(
        request_rows, VERIFIED_COUNT, KEY_HEADS, heads_per_key, HEAD_SIZE
    )
    request_keys = jnp.concatenate([prior_round_keys[0], new_keys[0]], axis=1).reshape(
        request_rows, 2 * VERIFIED_COUNT, KEY_HEADS, HEAD_SIZE
    )
    request_values = jnp.concatenate(
        [prior_round_values[0], verified_value_rows[0]], axis=1
    ).reshape(request_rows, 2 * VERIFIED_COUNT, KEY_HEADS, HEAD_SIZE)
    scores = (
        jnp.einsum(
            "rnkgd,rjkd->rkgnj", request_query, request_keys, preferred_element_type=jnp.float32
        )
        * score_scale
    )
    column = jnp.arange(2 * VERIFIED_COUNT, dtype=jnp.int32)
    position = jnp.arange(VERIFIED_COUNT, dtype=jnp.int32)
    live_prev = (column[None, :] < VERIFIED_COUNT) & (column[None, :] < accepted[0][:, None])
    live_new = (column[None, :] >= VERIFIED_COUNT) & (
        column[None, :] - VERIFIED_COUNT <= position[:, None]
    )
    live_rows = live_prev[:, None, None, None, :] | live_new[None, None, None, :, :]
    own_top, own_weights, own_mass = block_weights(scores, live_rows)
    own_part = jnp.einsum(
        "rkgnj,rjkd->rkgnd", own_weights, request_values, preferred_element_type=jnp.float32
    )
    own_flat = own_top.reshape(request_rows, row_lanes)
    best_top = jnp.maximum(got_top, own_flat)
    far_lift = jnp.exp(got_top - best_top)
    near_lift = jnp.exp(own_flat - best_top)
    overall_mass = far_lift * got_denominator + near_lift * own_mass.reshape(
        request_rows, row_lanes
    )
    overall_part = far_lift[..., None] * got_numerator.reshape(
        request_rows, row_lanes, HEAD_SIZE
    ) + near_lift[..., None] * own_part.reshape(request_rows, row_lanes, HEAD_SIZE)
    attention_output = (overall_part / overall_mass[..., None]).reshape(
        request_rows, KEY_HEADS, heads_per_key, VERIFIED_COUNT, HEAD_SIZE
    )
    return (
        attention_output.transpose(0, 3, 1, 2, 4)
        .reshape(1, request_rows, VERIFIED_COUNT, QUERY_HEADS * HEAD_SIZE)
        .astype(jnp.bfloat16)
    )


def solution(mesh):
    placed = (
        P("req", "blk", None, None),
        P("req", "blk", None, None),
        P("req", "blk", None, None),
        P("req", "blk", None, None),
        P("req", "blk", None, None),
        P("req", "blk"),
        P("req", None),
        P("req", None),
        P("req", None),
        P("req", "blk", None, None),
        P("req", "blk", None, None),
        P("req", "blk", None),
        P("req", "blk", None),
        P("req", "blk"),
    )
    return jax.shard_map(
        per_device,
        mesh=mesh,
        in_specs=placed,
        out_specs=P("req", "blk", None, None),
        check_vma=False,
    )
```

profile of v0, /device:TPU:0, one launch (start us, length us, event | category | flops | bytes accessed | tf_op | source)
XLA Modules:
  0.0 155.7 jit_solution(5203253228424417421)
XLA Ops:
  6.5 0.7 copy-done.18
  10.7 13.4 %all-reduce = bf16[16]{0:T(256)(128)(2,1)S(1)} all-reduce(bf16[16]{0:T(256)(128)(2,1)S(1)} %dynamic-update-slice), channel_id=2, replica_groups=mesh['blk'=8,'req'=4] {'req'}, use_global_device_ids=true, to_apply=%add | all-reduce | flops 16 | bytes 64 | tf_op jit(solution)/shard_map/all_gather | solution.py:76
  25.4 0.8 gather_fusion
  26.3 9.3 %all_gather.12 = bf16[1,16,5,1024]{3,2,0,1:T(8,128)(2,1)S(1)} all-gather(bf16[1,2,5,1024]{3,2,0,1:T(8,128)(2,1)S(1)} %copy.55), channel_id=1, replica_groups=mesh['blk'=8,'req'=4] {'blk'}, dimensions={1}, use_global_device_ids=true | all-gather | bytes 184320 | tf_op jit(solution)/shard_map/all_gather | solution.py:45
  36.6 14.4 %all_gather.14 = bf16[16,32,256]{2,1,0:T(8,128)(2,1)S(1)} all-gather(bf16[4,32,256]{2,1,0:T(8,128)(2,1)S(1)} %copy-done.8), channel_id=1, replica_groups=mesh['blk'=8,'req'=4] {'req'}, dimensions={0}, use_global_device_ids=true | all-gather | bytes 327680 | tf_op jit(solution)/shard_map/all_gather | solution.py:74
  51.8 0.7 gather_fusion.1
  52.5 1.5 fusion.40
  55.5 12.2 %pmax.7 = f32[16,80]{1,0:T(8,128)S(1)} all-reduce(f32[16,80]{1,0:T(8,128)S(1)} %max.18), channel_id=1, replica_groups=mesh['blk'=8,'req'=4] {'blk'}, use_global_device_ids=true, to_apply=%region_5.6 | all-reduce | flops 1280 | bytes 10240 | tf_op jit(solution)/shard_map/pmax | solution.py:101
  68.3 1.1 gather_fusion.4
  69.5 14.4 %all_gather.15 = bf16[16,32,256]{2,1,0:T(8,128)(2,1)S(1)} all-gather(bf16[4,32,256]{2,1,0:T(8,128)(2,1)S(1)} %copy-done.9), channel_id=1, replica_groups=mesh['blk'=8,'req'=4] {'req'}, dimensions={0}, use_global_device_ids=true | all-gather | bytes 327680 | tf_op jit(solution)/shard_map/all_gather | solution.py:75
  84.4 1.1 reshape.310
  86.1 1.7 %fusion.10 = f32[16,4,4,5,64]{4,3,2,1,0:T(8,128)S(1)} fusion(bf16[16,32,4,64,1]{3,2,1,0,4:T(4,128)(2,1)} %bitcast.77, f32[16,4,4,5,32]{4,3,2,1,0:T(8,128)S(1)} %copy-done.1, f32[16,4,4,5]{3,2,1,0:T(4,128)} %copy-done.4, pred[16]{0:T(512)(128)(4,1)S(1)} %copy-done.22), kind=kOutput, calls=%fused_computation.26 | convolution fusion | flops 5365760 | bytes 758800 | tf_op jit(solution)/shard_map/rkgnj,rjkd->rkgnd/dot_general | solution.py:92
  89.8 1.5 copy.66
  92.5 0.8 reshape.309
  93.3 2.1 %convolution_add_fusion = f32[16,5120]{1,0:T(8,128)} fusion(f32[16,5120]{1,0:T(8,128)S(1)} %mul.110, f32[16,5120]{1,0:T(8,128)S(1)} %reshape.311, f32[8,5120]{1,0:T(8,128)S(1)} %mul.107, f32[8,5120]{1,0:T(8,128)} %reshape.309, s32[8]{0:T(128)S(1)} %copy-done.20), kind=kOutput, calls=%fused_computation.6 | convolution fusion | flops 8069248 | bytes 1310752 | tf_op jit(solution)/shard_map/dot_general | solution.py:107
  96.7 0.8 convert_reduce_fusion
  98.0 0.7 copy-done.14
  98.8 0.7 copy-done.15
  99.5 0.7 copy-done.16
  100.3 0.7 copy-done.17
  103.1 12.1 %all-reduce.2 = f32[16,80]{1,0:T(8,128)S(1)} all-reduce(f32[16,80]{1,0:T(8,128)S(1)} %convolution_add_fusion.1), channel_id=4, replica_groups=mesh['blk'=8,'req'=4] {'blk'}, use_global_device_ids=true, to_apply=%region_10.11.clone | all-reduce | flops 1280 | bytes 10240
  117.4 29.5 %all-reduce.5.cloned.1.call-done = f32[16,5120]{1,0:T(8,128)} async-done(((f32[16,5120]{1,0:T(8,128)}), f32[16,5120]{1,0:T(8,128)}) %all-reduce.5.cloned.1.call-update) | async-done | bytes 327696
  146.8 0.9 constant_dynamic-slice_fusion
  148.1 0.7 convert_element_type.56
  (126 shorter events, 18.3 us)
Async XLA Ops:
  6.5 18.8 %copy-start = (s32[1,16]{1,0:T(1,128)S(1)}, s32[1,16]{1,0:T(1,128)}, u32[]{:S(2)}) copy-start(s32[1,16]{1,0:T(1,128)} %param.21) | copy-start | bytes 196
  6.5 140.3 %all-reduce.5.cloned.1.call-start = ((), (), s32[]{:S(2)}) async-start(), calls=%async_computation | async-start | bytes 655360
  6.5 0.7 copy-start.18
  7.9 16.3 %copy-start.19 = (s32[8]{0:T(128)}, s32[8]{0:T(128)S(1)}, u32[]{:S(2)}) copy-start(s32[8]{0:T(128)S(1)} %fusion.33) | copy-start | bytes 100
  24.3 0.7 copy-start.6
  24.9 27.6 %copy-start.21 = (pred[16]{0:T(512)(128)(4,1)}, pred[16]{0:T(512)(128)(4,1)S(1)}, u32[]{:S(2)}) copy-start(pred[16]{0:T(512)(128)(4,1)S(1)} %broadcast_compare_fusion) | copy-start | bytes 52
  26.3 28.4 %copy-start.11 = (pred[8,256]{1,0:T(8,128)(4,1)}, pred[8,256]{1,0:T(8,128)(4,1)S(1)}, u32[]{:S(2)}) copy-start(pred[8,256]{1,0:T(8,128)(4,1)S(1)} %iota_compare_fusion.1) | copy-start | bytes 6148
  35.7 0.8 copy-start.8
  52.5 1.6 %copy-start.3 = (bf16[1,8,256,256]{3,2,1,0:T(8,128)(2,1)S(1)}, bf16[1,8,256,256]{3,2,1,0:T(8,128)(2,1)}, u32[]{:S(2)}) copy-start(bf16[1,8,256,256]{3,2,1,0:T(8,128)(2,1)} %param.23) | copy-start | bytes 3145732
  54.0 0.7 copy-start.4
  54.7 14.8 %copy-start.9 = (bf16[4,32,256]{2,1,0:T(8,128)(2,1)S(1)}, bf16[4,32,256]{2,1,0:T(8,128)(2,1)}, u32[]{:S(2)}) copy-start(bf16[4,32,256]{2,1,0:T(8,128)(2,1)} %param.26) | copy-start | bytes 196612
  55.2 30.3 %copy-start.1 = (f32[16,4,4,5,32]{4,3,2,1,0:T(8,128)S(1)}, f32[16,4,4,5,32]{4,3,2,1,0:T(8,128)}, u32[]{:S(2)}) copy-start(f32[16,4,4,5,32]{4,3,2,1,0:T(8,128)} %get-tuple-element.9) | copy-start | bytes 491524
  87.8 0.7 copy-start.13
  88.7 0.7 copy-start.10
  91.3 0.7 copy-start.12
  92.0 1.3 copy-start.20
  92.5 3.7 %copy-start.2 = (f32[16,4,4,5,32]{4,3,2,1,0:T(8,128)S(1)}, f32[16,4,4,5,32]{4,3,2,1,0:T(8,128)}, u32[]{:S(2)}) copy-start(f32[16,4,4,5,32]{4,3,2,1,0:T(8,128)} %get-tuple-element.9) | copy-start | bytes 491524
  95.3 0.7 copy-start.7
  95.3 0.9 copy-start.5
  98.0 0.7 copy-start.14
  98.7 0.7 copy-start.15
  99.5 0.7 copy-start.16
  100.3 0.7 copy-start.17
  115.1 0.7 copy-start.27
  (6 other events, 3.9 us)
Sparse Core Ops, SparseCore 0:
  95.5 51.2 all-reduce.4
where the time goes:
time: 156 us
  blocking collectives  75.9 us (49%)
  waiting for transfers between devices  29.5 us (19%)
  local copies, waits for them, and re-layouts  25.3 us (16%)
  between operations  15.1 us (10%)
  matrix products  7 us (4%)
  other arithmetic  2.93 us (2%)
    unnamed x2, waiting for transfers between devices  29.5 us
    unnamed x66, local copies, waits for them, and re-layouts  15 us
    all_gather x1, blocking collectives, per_device(): lax.all_gather(shared_prompt_keys, 'req', axis=0, tiled=True)  14.4 us
    all_gather x1, blocking collectives, per_device(): lax.all_gather(shared_prompt_values, 'req', axis=0, tiled=True)  14.4 us
    all_gather x1, blocking collectives, per_device(): lax.all_gather(prompt_mask[:, 0].astype(jnp.bfloat16), 'req', axis=0, til...  13.4 us
    pmax x1, blocking collectives, per_device(): overall_top = lax.pmax(device_top, 'blk')  12.2 us
    unnamed x1, blocking collectives  12.1 us
    all_gather x1, blocking collectives, per_device(): lax.all_gather(verified_queries, 'blk', axis=1, tiled=True)[0]  9.31 us
  transfers between devices with their start and end apart: 1, of which 1 were waited for; matrix products, arithmetic and copies ran while one was open for 3% of the time, Pallas kernels for 0%

commit v1 on v0

--- a/solution.py
+++ b/solution.py
@@ -8,6 +8,28 @@
 HEAD_SIZE = 64
 VERIFIED_COUNT = 5
 LOWEST = -1e30
+
+
+def in_order(blocks, dim):
+    blocks = jnp.moveaxis(blocks, 0, dim)
+    lengths = blocks.shape
+    return blocks.reshape(*lengths[:dim], lengths[dim] * lengths[dim + 1], *lengths[dim + 2 :])
+
+
+def doubled(x, axis):
+    count = lax.axis_size(axis)
+    blocks = x[None]
+    for level in range(count.bit_length() - 1):
+        stride = 1 << level
+        other = lax.ppermute(blocks, axis, [(i, i ^ stride) for i in range(count)])
+        both = jnp.stack([blocks, other])
+        upper = lax.axis_index(axis) >> level & 1
+        blocks = jnp.where(upper == 0, both, both[::-1]).reshape(-1, *x.shape)
+    return blocks
+
+
+def gather_by_bits(x, axis, dim):
+    return in_order(doubled(x, axis), dim)
 
 
 def block_weights(scores, live_rows):
@@ -42,7 +64,7 @@
     score_scale = HEAD_SIZE ** (-0.5)
     row_lanes = QUERY_HEADS * VERIFIED_COUNT
     highest = lax.Precision.HIGHEST
-    every_query = lax.all_gather(verified_queries, "blk", axis=1, tiled=True)[0].reshape(
+    every_query = gather_by_bits(verified_queries, "blk", 1)[0].reshape(
         rows_of_batch, VERIFIED_COUNT, KEY_HEADS, heads_per_key, HEAD_SIZE
     )
     owners = slot_owner[0]

time: 156 us -> 179 us (1.15)
  waiting for transfers between devices: 29.5 us -> 52.8 us
  blocking collectives: 75.9 us -> 65.9 us
  starting transfers between devices: 0.01 us -> 3.6 us
  local copies, waits for them, and re-layouts: 25.3 us -> 28.7 us
  other arithmetic: 2.93 us -> 4.86 us
    unnamed x2, waiting for transfers between devices: 29.5 us -> 49.9 us
    all_gather x1 -> x0, blocking collectives: 9.31 us -> none  [per_device(): lax.all_gather(verified_queries, 'blk', axis=1, tiled=True)[0]]
    ppermute x0 -> x3, starting transfers between devices: none -> 3.6 us  [doubled(): other = lax.ppermute(blocks, axis, [(i, i ^ stride) for i in range(count)])]
    ppermute x0 -> x3, waiting for transfers between devices: none -> 2.92 us  [doubled(): other = lax.ppermute(blocks, axis, [(i, i ^ stride) for i in range(count)])]
    unnamed x66 -> x67, local copies, waits for them, and re-layouts: 15 us -> 15.8 us
  transfers between devices with their start and end apart: 1 -> 4, of which waited for: 1 -> 2; matrix products, arithmetic and copies ran while one was open for 3% -> 7% of each run, Pallas kernels for 0% -> 0%
where the time goes in v1:
time: 179 us; the launch traced here: 178 us
  blocking collectives  65.9 us (37%)
  waiting for transfers between devices  52.8 us (29%)
  local copies, waits for them, and re-layouts  28.7 us (16%)
  between operations  15.1 us (8%)
  matrix products  6.95 us (4%)
  other arithmetic  4.86 us (3%)
  starting transfers between devices  3.6 us (2%)
    unnamed x2, waiting for transfers between devices  49.9 us
    unnamed x67, local copies, waits for them, and re-layouts  15.8 us
    all_gather x1, blocking collectives, per_device(): lax.all_gather(shared_prompt_values, 'req', axis=0, tiled=True)  14.3 us
    all_gather x1, blocking collectives, per_device(): lax.all_gather(shared_prompt_keys, 'req', axis=0, tiled=True)  13.8 us
    all_gather x1, blocking collectives, per_device(): lax.all_gather(prompt_mask[:, 0].astype(jnp.bfloat16), 'req', axis=0, til...  13 us
    unnamed x1, blocking collectives  12.6 us
    pmax x1, blocking collectives, per_device(): overall_top = lax.pmax(device_top, 'blk')  12.2 us
    ppermute x3, starting transfers between devices, doubled(): other = lax.ppermute(blocks, axis, [(i, i ^ stride) for i in range(count)])  3.6 us
  transfers between devices with their start and end apart: 4, of which 2 were waited for; matrix products, arithmetic and copies ran while one was open for 7% of the time, Pallas kernels for 0%

profile of v1, /device:TPU:0, one launch (start us, length us, event | category | flops | bytes accessed | tf_op | source)
XLA Modules:
  0.0 177.9 jit_solution(8978116276390751210)
XLA Ops:
  11.4 13.0 %all-reduce = bf16[16]{0:T(256)(128)(2,1)S(1)} all-reduce(bf16[16]{0:T(256)(128)(2,1)S(1)} %dynamic-update-slice), channel_id=2, replica_groups=mesh['blk'=8,'req'=4] {'req'}, use_global_device_ids=true, to_apply=%add | all-reduce | flops 16 | bytes 64 | tf_op jit(solution)/shard_map/all_gather | solution.py:98
  27.1 0.8 gather_fusion
  30.5 13.8 %all_gather.10 = bf16[16,32,256]{2,1,0:T(8,128)(2,1)S(1)} all-gather(bf16[4,32,256]{2,1,0:T(8,128)(2,1)S(1)} %copy-done.10), channel_id=1, replica_groups=mesh['blk'=8,'req'=4] {'req'}, dimensions={0}, use_global_device_ids=true | all-gather | bytes 327680 | tf_op jit(solution)/shard_map/all_gather | solution.py:96
  44.4 1.6 collective-permute-start.1
  46.0 14.3 %all_gather.11 = bf16[16,32,256]{2,1,0:T(8,128)(2,1)S(1)} all-gather(bf16[4,32,256]{2,1,0:T(8,128)(2,1)S(1)} %copy-done.11), channel_id=1, replica_groups=mesh['blk'=8,'req'=4] {'req'}, dimensions={0}, use_global_device_ids=true | all-gather | bytes 327680 | tf_op jit(solution)/shard_map/all_gather | solution.py:97
  63.8 1.0 reshape.314
  65.4 1.0 reshape.318
  67.0 1.5 copy.68
  70.5 1.6 collective-permute-start.2
  72.1 2.9 %collective-permute-done.2 = bf16[4,1,2,5,1024]{4,2,0,3,1:T(2,128)(2,1)S(1)} collective-permute-done((bf16[4,1,2,5,1024]{4,2,0,3,1:T(2,128)(2,1)S(1)}, bf16[4,1,2,5,1024]{4,2,0,3,1:T(2,128)(2,1)S(1)}, u32[]{:S(2)}, u32[]{:S(2)}) %collective-permute-start.2) | collective-permute-done | bytes 81952 | tf_op jit(solution)/shard_map/ppermute | solution.py:24
  75.6 0.7 gather_fusion.1
  76.4 1.4 fusion.42
  79.2 12.2 %pmax.7 = f32[16,80]{1,0:T(8,128)S(1)} all-reduce(f32[16,80]{1,0:T(8,128)S(1)} %max.18), channel_id=1, replica_groups=mesh['blk'=8,'req'=4] {'blk'}, use_global_device_ids=true, to_apply=%region_5.6 | all-reduce | flops 1280 | bytes 10240 | tf_op jit(solution)/shard_map/pmax | solution.py:123
  92.0 2.0 %convert_reduce_fusion = f32[16,4,4,5]{3,2,1,0:T(4,128)S(1)} fusion(f32[16,4,4,5,32]{4,3,2,1,0:T(8,128)} %get-tuple-element.11, f32[16,4,4,5]{3,2,1,0:T(4,128)} %copy-done.4, pred[16]{0:T(512)(128)(4,1)} %copy-done.23), kind=kLoop, calls=%fused_computation.22 | loop fusion | flops 203520 | bytes 174096 | tf_op jit(solution)/shard_map/reduce_sum | solution.py:39
  94.7 2.6 %fusion.10 = f32[16,4,4,5,64]{4,3,2,1,0:T(8,128)} fusion(bf16[16,32,4,64,1]{3,2,1,0,4:T(4,128)(2,1)} %bitcast.87, f32[16,4,4,5,32]{4,3,2,1,0:T(8,128)S(1)} %copy-done.1, f32[16,4,4,5]{3,2,1,0:T(4,128)S(1)} %copy-done.5, pred[16]{0:T(512)(128)(4,1)S(1)} %copy-done.24), kind=kOutput, calls=%fused_computation.26 | convolution fusion | flops 5365760 | bytes 758800 | tf_op jit(solution)/shard_map/rkgnj,rjkd->rkgnd/dot_general | solution.py:114
  97.3 1.5 reshape.319
  100.3 12.6 %all-reduce.2 = f32[16,80]{1,0:T(8,128)} all-reduce(f32[16,80]{1,0:T(8,128)S(1)} %convolution_add_fusion.1), channel_id=4, replica_groups=mesh['blk'=8,'req'=4] {'blk'}, use_global_device_ids=true, to_apply=%region_10.11.clone | all-reduce | flops 1280 | bytes 10240
  113.1 0.8 mul.107
  115.0 0.8 copy-done.3
  115.8 1.1 convolution_add_fusion
  117.6 0.7 fusion.31
  118.6 49.9 %all-reduce.5.cloned.1.call-done = f32[16,5120]{1,0:T(8,128)} async-done(((f32[16,5120]{1,0:T(8,128)}), f32[16,5120]{1,0:T(8,128)}) %all-reduce.5.cloned.1.call-update) | async-done | bytes 327696
  168.5 0.9 constant_dynamic-slice_fusion
  170.4 0.7 convert_element_type.56
  (138 shorter events, 23.3 us)
Async XLA Ops:
  6.5 20.5 %copy-start = (s32[1,16]{1,0:T(1,128)S(1)}, s32[1,16]{1,0:T(1,128)}, u32[]{:S(2)}) copy-start(s32[1,16]{1,0:T(1,128)} %param.21) | copy-start | bytes 196
  6.5 162.0 %all-reduce.5.cloned.1.call-start = ((), (), s32[]{:S(2)}) async-start(), calls=%async_computation | async-start | bytes 655360
  6.5 37.8 %collective-permute-start = (bf16[1,1,2,5,1024]{4,2,3,1,0:T(2,128)(2,1)}, bf16[1,1,2,5,1024]{4,2,3,1,0:T(2,128)(2,1)S(1)}, u32[]{:S(2)}, u32[]{:S(2)}) collective-permute-start(bf16[1,1,2,5,1024]{4,2,3,1,0:T(2,128)(2,1)} %bitcast.90), channel_id=1, source_target_pairs={{0,4},{4,0},{8,12},{12,8},{16,20},{20,16},{24,28},{28,24},{1,5},{5... | collective-permute-start | bytes 61448 | tf_op jit(solution)/shard_map/ppermute | solution.py:24
  7.0 4.3 %copy-start.9 = (bf16[1,2,5,1024]{3,1,2,0:T(2,128)(2,1)S(1)}, bf16[1,2,5,1024]{3,1,2,0:T(2,128)(2,1)}, u32[]{:S(2)}) copy-start(bf16[1,2,5,1024]{3,1,2,0:T(2,128)(2,1)} %param.14) | copy-start | bytes 61444
  7.7 16.6 %copy-start.21 = (s32[8]{0:T(128)}, s32[8]{0:T(128)S(1)}, u32[]{:S(2)}) copy-start(s32[8]{0:T(128)S(1)} %fusion.35) | copy-start | bytes 100
  7.8 0.7 copy-start.25
  25.1 0.7 copy-start.14
  25.1 51.2 %copy-start.23 = (pred[16]{0:T(512)(128)(4,1)}, pred[16]{0:T(512)(128)(4,1)S(1)}, u32[]{:S(2)}) copy-start(pred[16]{0:T(512)(128)(4,1)S(1)} %broadcast_compare_fusion) | copy-start | bytes 52
  25.9 0.7 copy-start.15
  29.7 0.8 copy-start.10
  44.4 1.6 copy-start.11
  44.4 25.8 %collective-permute-start.1 = (bf16[2,1,2,5,1024]{4,2,3,0,1:T(2,128)(2,1)S(1)}, bf16[2,1,2,5,1024]{4,2,3,0,1:T(2,128)(2,1)S(1)}, u32[]{:S(2)}, u32[]{:S(2)}) collective-permute-start(bf16[2,1,2,5,1024]{4,2,3,0,1:T(2,128)(2,1)S(1)} %get-tuple-element.9), channel_id=1, source_target_pairs={{0,8},{4,12},{8,0},{12,4},{16,24},{20,28},{24,16},{28,20},{1,9},{5... | collective-permute-start | bytes 122888 | tf_op jit(solution)/shard_map/ppermute | solution.py:24
  61.0 0.7 copy-start.16
  61.8 0.7 copy-start.17
  63.8 2.7 %copy-start.2 = (bf16[1,8,256,256]{3,2,1,0:T(8,128)(2,1)S(1)}, bf16[1,8,256,256]{3,2,1,0:T(8,128)(2,1)}, u32[]{:S(2)}) copy-start(bf16[1,8,256,256]{3,2,1,0:T(8,128)(2,1)} %param.23) | copy-start | bytes 3145732
  68.5 0.7 copy-start.28
  70.5 4.5 %collective-permute-start.2 = (bf16[4,1,2,5,1024]{4,2,0,3,1:T(2,128)(2,1)S(1)}, bf16[4,1,2,5,1024]{4,2,0,3,1:T(2,128)(2,1)S(1)}, u32[]{:S(2)}, u32[]{:S(2)}) collective-permute-start(bf16[4,1,2,5,1024]{4,2,0,3,1:T(2,128)(2,1)S(1)} %copy.57), channel_id=1, source_target_pairs={{0,16},{4,20},{8,24},{12,28},{16,0},{20,4},{24,8},{28,12},{1,17},{... | collective-permute-start | bytes 245768 | tf_op jit(solution)/shard_map/ppermute | solution.py:24
  75.2 1.1 copy-start.6
  79.0 15.1 %copy-start.1 = (f32[16,4,4,5,32]{4,3,2,1,0:T(8,128)S(1)}, f32[16,4,4,5,32]{4,3,2,1,0:T(8,128)}, u32[]{:S(2)}) copy-start(f32[16,4,4,5,32]{4,3,2,1,0:T(8,128)} %get-tuple-element.11) | copy-start | bytes 491524
  92.0 2.1 %copy-start.5 = (f32[16,4,4,5]{3,2,1,0:T(4,128)S(1)}, f32[16,4,4,5]{3,2,1,0:T(4,128)}, u32[]{:S(2)}) copy-start(f32[16,4,4,5]{3,2,1,0:T(4,128)} %copy-done.4) | copy-start | bytes 15364
  114.9 0.9 copy-start.3
  116.9 0.7 copy-start.18
  116.9 0.7 copy-start.19
  118.6 51.0 %copy-start.8 = (f32[2,4,4,5,10]{4,3,2,1,0:T(8,128)S(1)}, f32[2,4,4,5,10]{4,3,2,1,0:T(8,128)}, u32[]{:S(2)}) copy-start(f32[2,4,4,5,10]{4,3,2,1,0:T(8,128)} %copy-done.7) | copy-start | bytes 19204
  (10 other events, 6.4 us)
Sparse Core Ops, SparseCore 0:
  117.1 51.3 all-reduce.4
